TPU v7x, 32 devices: a whole 2x2x4 slice. The times are simulated.
32 devices in a mesh: row: 8 (over z, x), col: 4 (over y, core).
Axes of the slice: x: 2, y: 2, z: 4, core: 2. Of those that a mesh axis runs over, the one named last changes fastest.
Arguments:
- features: float32 [136, 8192], P(None, 'row'), may hold values from -6 to 6
- factor: float32 [8192, 16384], P('row', 'col')
Outputs:
- panel: float32 [8192, 512], P(('row', 'col'))
All inputs are finite; a program needn't handle non-finite values.
Results may differ from a plain program's by a relative error of at most 0.000067.
Values sent between devices are 32-bit elements; how exact they have to be, the bound alone decides.
No kernel may reach another device: no remote copies, remote signals or barrier semaphores. Data moves between devices by JAX's collectives and lax.ppermute only.
A program may use at most 128 MiB of HBM per device.

v0:
```python
import jax
import jax.numpy as jnp
from jax import lax
from jax.sharding import PartitionSpec as P

B = 512
ridge_value = 40.0


def broadcast(x, axis, root):
    mine = lax.axis_index(axis) == root
    return lax.psum(jnp.where(mine, x, jnp.zeros_like(x)), axis)


def kernel(points, anchors):
    feature_count = points.shape[0]
    products = lax.dot_general(
        points,
        anchors,
        (((0,), (0,)), ((), ())),
        precision=lax.Precision.HIGHEST,
        preferred_element_type=jnp.float32,
    )
    norm_points = jnp.sum(points * points, axis=0)
    norm_anchors = jnp.sum(anchors * anchors, axis=0)
    distance = norm_points[:, None] + norm_anchors[None, :] - 2.0 * products
    return products / feature_count + jnp.exp(-distance / (2.0 * feature_count))


def times_rows(block, pivot_factor):
    return lax.dot_general(
        block,
        pivot_factor,
        (((1,), (1,)), ((), ())),
        precision=lax.Precision.HIGHEST,
        preferred_element_type=jnp.float32,
    )


def on_device(features, factor):
    rows_dev = factor.shape[0]
    slab_rows = rows_dev // lax.axis_size("col")
    col_index = lax.axis_index("col")
    row_index = lax.axis_index("row")
    pivot_factor, pivot_points = (
        broadcast(factor[:B], "row", 0),
        broadcast(features[:, :B], "row", 0),
    )
    own_points = lax.dynamic_slice_in_dim(features, col_index * slab_rows, slab_rows, 1)
    global_rows = row_index * rows_dev + col_index * slab_rows + lax.iota(jnp.int32, slab_rows)
    identity_rows = (global_rows[:, None] == lax.iota(jnp.int32, B)[None, :]).astype(jnp.float32)
    slab_kernel = kernel(own_points, pivot_points) + ridge_value * identity_rows
    local_sums = lax.psum_scatter(
        times_rows(factor, pivot_factor), "col", scatter_dimension=0, tiled=True
    )
    pivot_kernel = kernel(pivot_points, pivot_points) + ridge_value * jnp.eye(B, dtype=jnp.float32)
    gram_sums = lax.psum(times_rows(pivot_factor, pivot_factor), "col")
    lower_factor = jnp.linalg.cholesky(pivot_kernel - gram_sums)
    slab_values = slab_kernel - local_sums
    solved = jax.scipy.linalg.solve_triangular(lower_factor, slab_values.T, lower=True)
    return solved.T


def solution(mesh):
    placed = (P(None, "row"), P("row", "col"))
    return jax.shard_map(
        on_device, mesh=mesh, in_specs=placed, out_specs=P(("row", "col"), None), check_vma=False
    )
```

profile of v0, /device:TPU:0, one launch (start us, length us, event | category | flops | bytes accessed | tf_op | source)
XLA Modules:
  0.0 500.9 jit_solution(18310001285476813310)
XLA Ops:
  6.5 7.7 %slice_select_fusion = f32[512,4096]{1,0:T(8,128)} fusion(f32[1024,4096]{1,0:T(8,128)} %param.3, pred[]{:T(512)S(6)} %eq.20), kind=kLoop, calls=%fused_computation.2 | loop fusion | flops 2097152 | bytes 16777216 | tf_op jit(solution)/shard_map/jit(_where)/select_n | solution.py:12
  14.3 0.7 slice_select_fusion.1
  15.1 280.9 %all-reduce.7.cloned.1.call-done = (f32[512,4096]{1,0:T(8,128)}, f32[136,512]{1,0:T(8,128)}) async-done(((f32[512,4096]{1,0:T(8,128)}, f32[136,512]{1,0:T(8,128)}), (f32[512,4096]{1,0:T(8,128)}, f32[136,512]{1,0:T(8,128)})) %all-reduce.7.cloned.1.call-update) | async-done | bytes 8667152 | tf_op jit(solution)/shard_map/psum | solution.py:12
  296.0 17.2 %fusion.33 = f32[512,512]{0,1:T(8,128)} fusion(f32[512,4096]{1,0:T(8,128)} %get-tuple-element.25), kind=kOutput, calls=%fused_computation.79 | convolution fusion | flops 12884901888 | bytes 9437184 | tf_op jit(solution)/shard_map/dot_general | solution.py:31
  313.3 31.7 %convolution_bitcast_fusion = f32[1024,512]{1,0:T(8,128)} fusion(f32[512,4096]{1,0:T(8,128)} %get-tuple-element.25, f32[1024,4096]{1,0:T(8,128)} %param.3), kind=kOutput, calls=%fused_computation.3 | convolution fusion | flops 25769803776 | bytes 27262976 | tf_op jit(solution)/shard_map/dot_general | solution.py:31
  345.0 3.8 all-reduce.5.cloned.1.call-done
  348.8 2.6 add_subtract_fusion
  351.4 0.3 copy.6
  351.7 0.2 fusion
  352.0 11.7 %cholesky.103 = f32[128,128]{1,0:T(8,128)S(1)} custom-call(f32[128,128]{1,0:T(8,128)S(1)} %cholesky.263), custom_call_target="Cholesky" | custom-call | tf_op jit(solution)/shard_map/jit(cholesky)/cholesky | solution.py:58
  363.7 9.8 %custom-call.31 = f32[1,128,128]{1,2,0:T(8,128)S(1)} custom-call(f32[1,128,128]{2,1,0:T(8,128)S(1)} %get-tuple-element.34), custom_call_target="InvertDiagBlocksLowerTriangular" | custom-call | tf_op jit(solution)/shard_map/jit(cholesky)/cholesky | solution.py:58
  373.6 0.3 fusion.12
  373.9 0.3 convolution_subtract_fusion
  374.5 11.9 %cholesky.215 = f32[128,128]{1,0:T(8,128)S(1)} custom-call(f32[128,128]{1,0:T(8,128)S(1)} %cholesky.267), custom_call_target="Cholesky" | custom-call | tf_op jit(solution)/shard_map/jit(cholesky)/cholesky | solution.py:58
  386.5 9.8 %custom-call.32 = f32[1,128,128]{1,2,0:T(8,128)S(1)} custom-call(f32[1,128,128]{2,1,0:T(8,128)S(1)} %get-tuple-element.32), custom_call_target="InvertDiagBlocksLowerTriangular" | custom-call | tf_op jit(solution)/shard_map/jit(cholesky)/cholesky | solution.py:58
  396.4 0.3 convolution_dynamic-update-slice_fusion
  396.8 0.6 convolution_subtract_fusion.3
  397.4 11.7 %cholesky.236 = f32[128,128]{1,0:T(8,128)S(1)} custom-call(f32[128,128]{1,0:T(8,128)S(1)} %cholesky.272), custom_call_target="Cholesky" | custom-call | tf_op jit(solution)/shard_map/jit(cholesky)/cholesky | solution.py:58
  409.2 9.8 %custom-call.33 = f32[1,128,128]{1,2,0:T(8,128)S(1)} custom-call(f32[1,128,128]{2,1,0:T(8,128)S(1)} %get-tuple-element.30), custom_call_target="InvertDiagBlocksLowerTriangular" | custom-call | tf_op jit(solution)/shard_map/jit(cholesky)/cholesky | solution.py:58
  419.0 0.3 convolution_dynamic-update-slice_fusion.1
  419.3 0.5 convolution_subtract_fusion.5
  419.8 11.9 %cholesky.253 = f32[128,128]{1,0:T(8,128)S(1)} custom-call(f32[128,128]{1,0:T(8,128)S(1)} %convolution_subtract_fusion.5), custom_call_target="Cholesky" | custom-call | tf_op jit(solution)/shard_map/jit(cholesky)/cholesky | solution.py:58
  431.9 0.7 compare_reduce_fusion.2
  433.9 0.6 compare_reduce_fusion.1
  435.2 0.6 compare_reduce_fusion
  436.7 11.2 %while.1 = (s32[]{:T(128)}, f32[512,512]{0,1:T(8,128)S(1)}, s32[4,2]{0,1:T(2,128)S(1)}, f32[4,128,128]{2,1,0:T(8,128)}, s32[]{:T(128)}) while((s32[]{:T(128)}, f32[512,512]{0,1:T(8,128)S(1)}, s32[4,2]{0,1:T(2,128)S(1)}, f32[4,128,128]{2,1,0:T(8,128)}, s32[]{:T(128)}) %tuple.24), condition=%wide.while_cond, body=%wide.while_body.sunk | while | flops 2 | bytes 393829 | solution.py:60
  436.8 0.6 fusion.47
  437.3 1.4 dynamic-slice.7
  438.8 0.6 bitcast_dynamic-update-slice_fusion.2
  439.5 0.6 fusion.47
  440.1 1.4 dynamic-slice.7
  441.6 0.6 bitcast_dynamic-update-slice_fusion.2
  442.3 0.6 fusion.47
  442.9 1.4 dynamic-slice.7
  444.4 0.6 bitcast_dynamic-update-slice_fusion.2
  445.1 0.6 fusion.47
  445.7 1.4 dynamic-slice.7
  447.2 0.6 bitcast_dynamic-update-slice_fusion.2
  447.8 40.1 %custom-call.34 = f32[4,128,128]{1,2,0:T(8,128)S(1)} custom-call(f32[4,128,128]{2,1,0:T(8,128)} %get-tuple-element.12), custom_call_target="InvertDiagBlocksLowerTriangular" | custom-call | tf_op jit(solution)/shard_map/jit(_solve_triangular)/triangular_solve | solution.py:60
  488.0 2.0 subtract_bitcast_fusion
  490.0 0.3 fusion.15
  490.3 0.4 convolution_subtract_fusion.4
  490.7 0.3 fusion.23
  491.0 0.6 convolution_subtract_fusion.2
  491.6 0.3 fusion.21
  491.9 0.8 convolution_subtract_fusion.1
  492.7 0.3 fusion.20
  493.1 1.0 copy.16
  (44 shorter events, 1.9 us)
Async XLA Ops:
  6.5 289.5 %all-reduce.7.cloned.1.call-start = ((), (), s32[]{:S(2)}) async-start(), calls=%async_computation.3 | async-start | bytes 17334272 | tf_op jit(solution)/shard_map/psum | solution.py:12
  6.5 7.7 %copy-start = (f32[136,1024]{1,0:T(8,128)S(1)}, f32[136,1024]{1,0:T(8,128)}, u32[]{:S(2)}) copy-start(f32[136,1024]{1,0:T(8,128)} %param.2) | copy-start | bytes 1671172
  15.0 333.8 %all-reduce.5.cloned.1.call-start = ((), (), s32[]{:S(2)}) async-start(), calls=%async_computation.1 | async-start | bytes 2097152 | tf_op jit(solution)/shard_map/psum | solution.py:57
  313.2 31.7 %copy-start.1 = (f32[136,512]{1,0:T(8,128)S(1)}, f32[136,512]{1,0:T(8,128)}, u32[]{:S(2)}) copy-start(f32[136,512]{1,0:T(8,128)} %get-tuple-element.26) | copy-start | bytes 835588
  313.2 174.7 %reduce-scatter.2.cloned.1.call-start = ((), (), s32[]{:S(2)}) async-start(), calls=%async_computation.2 | async-start | bytes 2621440 | tf_op jit(solution)/shard_map/reduce_scatter | solution.py:53
Sparse Core Ops, SparseCore 0:
  15.1 280.8 all-reduce.6
  313.4 35.3 all-reduce.4
  351.3 31.7 reduce-scatter.1
where the time goes:
time: 509 us; the launch traced here: 501 us
  waiting for transfers between devices  285 us (56%)
  other arithmetic  128 us (25%)
  matrix products  58.8 us (12%)
  between operations  16.3 us (3%)
  local copies, waits for them, and re-layouts  13.1 us (3%)
    psum x1, waiting for transfers between devices, broadcast(): return lax.psum(jnp.where(mine, x, jnp.zeros_like(x)), axis)  281 us
    another operation x14, other arithmetic, on_device(): lower_factor = jnp.linalg.cholesky(pivot_kernel - gram_sums)  78.7 us
    dot_general x2, matrix products, times_rows(): lax.dot_general(block, pivot_factor, (((1,), (1,)), ((), ())), precision=...  48.9 us
    another operation x3, other arithmetic, on_device(): jax.scipy.linalg.solve_triangular(lower_factor, slab_values.T, lower=True)  40.3 us
    another operation x20, local copies, waits for them, and re-layouts  11.1 us
  transfers between devices with their start and end apart: 3, of which 2 were waited for; matrix products, arithmetic and copies ran while one was open for 34% of the time, Pallas kernels for 0%

commit v1 on v0

--- a/solution.py
+++ b/solution.py
@@ -9,7 +9,7 @@
 
 def broadcast(x, axis, root):
     mine = lax.axis_index(axis) == root
-    return lax.psum(jnp.where(mine, x, jnp.zeros_like(x)), axis)
+    return jnp.sum(lax.all_gather(jnp.where(mine, x, jnp.zeros_like(x)), axis), axis=0)
 
 
 def kernel(points, anchors):

time: 509 us -> 1560 us (3.06)
  waiting for transfers between devices: 285 us -> 1320 us
  other arithmetic: 128 us -> 156 us
    all_gather x0 -> x2, waiting for transfers between devices: none -> 1310 us  [broadcast(): lax.all_gather(jnp.where(mine, x, jnp.zeros_like(x)), axis)]
    psum x1 -> x0, waiting for transfers between devices: 281 us -> none  [broadcast(): return lax.psum(jnp.where(mine, x, jnp.zeros_like(x)), axis)]
    reduce_sum x0 -> x2, other arithmetic: none -> 26.3 us  [broadcast(): jnp.sum(lax.all_gather(jnp.where(mine, x, jnp.zeros_like(x)), axis), axis=0)]
  transfers between devices with their start and end apart: 3 -> 4, of which waited for: 2 -> 3; matrix products, arithmetic and copies ran while one was open for 34% -> 11% of each run, Pallas kernels for 0% -> 0%
where the time goes in v1:
time: 1560 us
  waiting for transfers between devices  1320 us (85%)
  other arithmetic  156 us (10%)
  matrix products  58.5 us (4%)
  between operations  16.5 us (1%)
    all_gather x2, waiting for transfers between devices, broadcast(): lax.all_gather(jnp.where(mine, x, jnp.zeros_like(x)), axis)  1310 us
    another operation x14, other arithmetic, on_device(): lower_factor = jnp.linalg.cholesky(pivot_kernel - gram_sums)  78.7 us
    dot_general x2, matrix products, times_rows(): lax.dot_general(block, pivot_factor, (((1,), (1,)), ((), ())), precision=...  48.5 us
    another operation x3, other arithmetic, on_device(): jax.scipy.linalg.solve_triangular(lower_factor, slab_values.T, lower=True)  40.3 us
  transfers between devices with their start and end apart: 4, of which 3 were waited for; matrix products, arithmetic and copies ran while one was open for 11% of the time, Pallas kernels for 0%

profile of v1, /device:TPU:0, one launch (start us, length us, event | category | flops | bytes accessed | tf_op | source)
XLA Modules:
  0.0 1559.5 jit_solution(8521832374561182024)
XLA Ops:
  6.5 1.7 slice_select_fusion.1
  8.3 7.6 slice_select_fusion
  16.0 0.9 multiply_reduce_fusion.1
  17.0 45.7 %all-gather.5.cloned.1.call-done = f32[1088,512]{1,0:T(8,128)} async-done(((f32[136,512]{1,0:T(8,128)}), f32[1088,512]{1,0:T(8,128)}) %all-gather.5.cloned.1.call-update) | async-done | bytes 2228240 | tf_op jit(solution)/shard_map/all_gather | solution.py:12
  62.7 1.9 reduce_sum.35
  64.6 1265.0 %all-gather.7.cloned.1.call-done = f32[4096,4096]{1,0:T(8,128)} async-done(((f32[512,4096]{1,0:T(8,128)}), f32[4096,4096]{1,0:T(8,128)}) %all-gather.7.cloned.1.call-update) | async-done | bytes 67108880 | tf_op jit(solution)/shard_map/all_gather | solution.py:12
  1329.6 24.4 %reduce_sum.37 = f32[512,4096]{1,0:T(8,128)} reduce(f32[8,512,4096]{2,1,0:T(8,128)} %bitcast.1, f32[]{:T(128)} %constant.167.clone.1), dimensions={0}, to_apply=%region_2.3 | reduce | flops 14680064 | bytes 75497472 | tf_op jit(solution)/shard_map/reduce_sum | solution.py:12
  1354.0 17.2 %fusion.33 = f32[512,512]{0,1:T(8,128)} fusion(f32[512,4096]{1,0:T(8,128)} %reduce_sum.37), kind=kOutput, calls=%fused_computation.79 | convolution fusion | flops 12884901888 | bytes 9437184 | tf_op jit(solution)/shard_map/dot_general | solution.py:31
  1371.2 0.6 reduce-scatter.2.cloned.1.call-start
  1371.8 31.3 %convolution_bitcast_fusion = f32[1024,512]{1,0:T(8,128)} fusion(f32[512,4096]{1,0:T(8,128)} %reduce_sum.37, f32[1024,4096]{1,0:T(8,128)} %param.3), kind=kOutput, calls=%fused_computation.3 | convolution fusion | flops 25769803776 | bytes 27262976 | tf_op jit(solution)/shard_map/dot_general | solution.py:31
  1403.1 4.5 all-reduce.3.cloned.1.call-done
  1407.6 2.6 add_subtract_fusion
  1410.3 0.3 copy.20
  1410.8 11.7 cholesky.103
  1422.6 9.8 custom-call.31
  1432.7 0.3 convolution_subtract_fusion
  1433.4 11.9 cholesky.215
  1445.5 9.8 custom-call.32
  1455.3 0.3 convolution_dynamic-update-slice_fusion
  1455.6 0.6 convolution_subtract_fusion.3
  1456.3 11.7 cholesky.236
  1468.1 9.8 custom-call.33
  1478.2 0.5 convolution_subtract_fusion.5
  1478.7 11.9 cholesky.253
  1490.8 0.7 compare_reduce_fusion.2
  1492.7 0.6 compare_reduce_fusion.1
  1494.0 0.6 compare_reduce_fusion
  1495.5 10.8 while.1
  1495.5 0.5 fusion.47
  1496.1 1.4 dynamic-slice.7
  1497.5 0.6 bitcast_dynamic-update-slice_fusion.2
  1498.2 0.5 fusion.47
  1498.8 1.4 dynamic-slice.7
  1500.2 0.6 bitcast_dynamic-update-slice_fusion.2
  1500.9 0.5 fusion.47
  1501.4 1.4 dynamic-slice.7
  1502.9 0.6 bitcast_dynamic-update-slice_fusion.2
  1503.6 0.5 fusion.47
  1504.1 1.4 dynamic-slice.7
  1505.6 0.6 bitcast_dynamic-update-slice_fusion.2
  1506.2 40.1 %custom-call.34 = f32[4,128,128]{1,2,0:T(8,128)S(1)} custom-call(f32[4,128,128]{2,1,0:T(8,128)} %get-tuple-element.12), custom_call_target="InvertDiagBlocksLowerTriangular" | custom-call | tf_op jit(solution)/shard_map/jit(_solve_triangular)/triangular_solve | solution.py:60
  1546.4 2.0 subtract_bitcast_fusion
  1548.4 0.3 fusion.15
  1548.7 0.4 convolution_subtract_fusion.4
  1549.4 0.6 convolution_subtract_fusion.2
  1550.3 0.8 convolution_subtract_fusion.1
  1551.1 0.3 fusion.20
  1551.5 1.0 copy.30
  (45 shorter events, 3.3 us)
Async XLA Ops:
  6.5 56.1 %all-gather.5.cloned.1.call-start = ((), (), s32[]{:S(2)}) async-start(), calls=%async_computation.3 | async-start | bytes 2506752 | tf_op jit(solution)/shard_map/all_gather | solution.py:12
  8.2 1321.3 %all-gather.7.cloned.1.call-start = ((), (), s32[]{:S(2)}) async-start(), calls=%async_computation.4 | async-start | bytes 75497472 | tf_op jit(solution)/shard_map/all_gather | solution.py:12
  15.9 1391.7 %all-reduce.3.cloned.1.call-start = ((), (), s32[]{:S(2)}) async-start(), calls=%async_computation.1 | async-start | bytes 2097152 | tf_op jit(solution)/shard_map/psum | solution.py:57
  1371.2 175.1 %reduce-scatter.2.cloned.1.call-start = ((), (), s32[]{:S(2)}) async-start(), calls=%async_computation.2 | async-start | bytes 2621440 | tf_op jit(solution)/shard_map/reduce_scatter | solution.py:53
Sparse Core Ops, SparseCore 0:
  9.5 53.1 all-gather.4
  64.2 1265.3 all-gather.6
  1371.3 36.2 all-reduce.2
  1410.0 31.7 reduce-scatter.1
